TPU v7x, 32 devices: a whole 2x2x4 slice. The times are simulated.
32 devices in a mesh: dp: 2 (over core), ctx: 16 (over z, y, x).
Axes of the slice: x: 2, y: 2, z: 4, core: 2. Of those that a mesh axis runs over, the one named last changes fastest.
Arguments:
- layer_in: bfloat16 [2, 4096, 768], P('dp', 'ctx'), may hold values from -6 to 6
- out_grad: bfloat16 [2, 4096, 768], P('dp', 'ctx'), may hold values from -6 to 6
- first_gain: bfloat16 [768], P('dp'), may hold values from 0.099609375 to 1.8984375
- query_weight: bfloat16 [768, 768], P('dp'), may hold values from -0.21875 to 0.21875
- key_weight: bfloat16 [768, 768], P('dp'), may hold values from -0.21875 to 0.21875
- value_weight: bfloat16 [768, 768], P('dp'), may hold values from -0.21875 to 0.21875
- output_weight: bfloat16 [768, 768], P('dp'), may hold values from -6 to 6
- second_gain: bfloat16 [768], P('dp'), may hold values from 0.099609375 to 1.8984375
- gate_weight: bfloat16 [768, 2048], P('dp'), may hold values from -0.21875 to 0.21875
- up_weight: bfloat16 [768, 2048], P('dp'), may hold values from -0.21875 to 0.21875
- down_weight: bfloat16 [2048, 768], P('dp'), may hold values from -0.125 to 0.125
Outputs:
- layer_out: bfloat16 [2, 4096, 768], P('dp', 'ctx')
- in_grad: bfloat16 [2, 4096, 768], P('dp', 'ctx')
- first_gain_grad: float32 [768], P('dp')
- query_grad: float32 [768, 768], P('dp')
- key_grad: float32 [768, 768], P('dp')
- value_grad: float32 [768, 768], P('dp')
- output_grad: float32 [768, 768], P('dp')
- second_gain_grad: float32 [768], P('dp')
- gate_grad: float32 [768, 2048], P('dp')
- up_grad: float32 [768, 2048], P('dp')
- down_grad: float32 [2048, 768], P('dp')
All inputs are finite; a program needn't handle non-finite values.
Results may differ from a plain program's by a relative error of at most 0.02.
Values may be sent and summed in bfloat16 or wider, within the bound.
No kernel may reach another device: no remote copies, remote signals or barrier semaphores. Data moves between devices by JAX's collectives and lax.ppermute only.
A program may use at most 448 MiB of HBM per device.

v0:
```python
import jax
import jax.numpy as jnp
from jax import lax
from jax.sharding import PartitionSpec as P

HEADS = 12
HEAD_DIM = 64
EPS = 1e-06


def normed(rows, gain):
    return rows * lax.rsqrt(jnp.mean(rows * rows, axis=-1, keepdims=True) + EPS) * gain


def gated(gate, upper):
    return jax.nn.gelu(gate, approximate=True) * upper


def heads_of(rows):
    return rows.reshape(rows.shape[0], HEADS, HEAD_DIM)


def scores_of(query, keys):
    return jnp.einsum(
        "qhd,khd->hqk", heads_of(query), heads_of(keys), preferred_element_type=jnp.float32
    ) * HEAD_DIM ** (-0.5)


def attend(operands):
    query, keys, values = operands
    scores = scores_of(query, keys)
    top = jnp.max(scores, axis=-1, keepdims=True)
    expd = jnp.exp(scores - top)
    total = jnp.sum(expd, axis=-1, keepdims=True)
    probs = (expd / total).astype(jnp.bfloat16)
    mixed = jnp.einsum("hqk,khd->qhd", probs, heads_of(values), preferred_element_type=jnp.float32)
    mixed = mixed.reshape(query.shape[0], HEADS * HEAD_DIM).astype(jnp.bfloat16)
    return (mixed, (top + jnp.log(total))[..., 0])


def back_core(query, keys, values, grad_mix, logsum):
    probs = jnp.exp(scores_of(query, keys) - logsum[..., None])
    grad_prob = jnp.einsum(
        "qhd,khd->hqk", heads_of(grad_mix), heads_of(values), preferred_element_type=jnp.float32
    )
    delta = jnp.sum(grad_prob * probs, axis=-1)
    grad_score = (probs * (grad_prob - delta[..., None])).astype(jnp.bfloat16)
    return (probs, grad_score, delta)


def query_part(grad_score, keys, count):
    grad_query = jnp.einsum(
        "hqk,khd->qhd", grad_score, heads_of(keys), preferred_element_type=jnp.float32
    ) * HEAD_DIM ** (-0.5)
    return grad_query.reshape(count, HEADS * HEAD_DIM).astype(jnp.bfloat16)


def attend_back(operands):
    query, keys, values, grad_mix, logsum = operands
    probs, grad_score, delta = back_core(query, keys, values, grad_mix, logsum)
    grad_query = query_part(grad_score, keys, query.shape[0])
    grad_keys = jnp.einsum(
        "hqk,qhd->khd", grad_score, heads_of(query), preferred_element_type=jnp.float32
    ) * HEAD_DIM ** (-0.5)
    grad_values = jnp.einsum(
        "hqk,qhd->khd",
        probs.astype(jnp.bfloat16),
        heads_of(grad_mix),
        preferred_element_type=jnp.float32,
    )
    return (
        grad_query,
        grad_keys.reshape(keys.shape[0], -1),
        grad_values.reshape(keys.shape[0], -1),
    )


def product(left, right):
    return jnp.dot(left, right, preferred_element_type=jnp.float32)


def on_device(
    layer_in,
    out_grad,
    first_gain,
    query_weight,
    key_weight,
    value_weight,
    output_weight,
    second_gain,
    gate_weight,
    up_weight,
    down_weight,
):
    seqs, local, width = layer_in.shape
    rows = seqs * local

    def shaped(matrix):
        return matrix.reshape(seqs, local, width)

    gain_one, w_query, w_key, w_value, w_output = (
        lax.all_gather(first_gain, "dp", axis=0, tiled=True),
        lax.all_gather(query_weight, "dp", axis=0, tiled=True),
        lax.all_gather(key_weight, "dp", axis=0, tiled=True),
        lax.all_gather(value_weight, "dp", axis=0, tiled=True),
        lax.all_gather(output_weight, "dp", axis=0, tiled=True),
    )
    inputs = layer_in.reshape(rows, width).astype(jnp.float32)
    gain_one_f = gain_one.astype(jnp.float32)
    normal_one = normed(inputs, gain_one_f).astype(jnp.bfloat16)
    query = product(normal_one, w_query).astype(jnp.bfloat16)
    keys = product(normal_one, w_key).astype(jnp.bfloat16)
    values = product(normal_one, w_value).astype(jnp.bfloat16)
    keys_all, values_all = (
        lax.all_gather(shaped(keys), "ctx", axis=1, tiled=True),
        lax.all_gather(shaped(values), "ctx", axis=1, tiled=True),
    )
    mixed, logsum = lax.map(attend, (shaped(query), keys_all, values_all))
    mixed_rows = mixed.reshape(rows, width)
    middle = inputs + product(mixed_rows, w_output)
    gain_two, w_gate, w_up, w_down = (
        lax.all_gather(second_gain, "dp", axis=0, tiled=True),
        lax.all_gather(gate_weight, "dp", axis=0, tiled=True),
        lax.all_gather(up_weight, "dp", axis=0, tiled=True),
        lax.all_gather(down_weight, "dp", axis=0, tiled=True),
    )
    gain_two_f = gain_two.astype(jnp.float32)
    normal_two = normed(middle, gain_two_f).astype(jnp.bfloat16)
    gate = product(normal_two, w_gate)
    upper = product(normal_two, w_up)
    hidden = gated(gate, upper).astype(jnp.bfloat16)
    result = middle + product(hidden, w_down)
    layer_out = result.astype(jnp.bfloat16).reshape(seqs, local, width)
    gain_one, w_query, w_key, w_value, w_output = (
        lax.all_gather(first_gain, "dp", axis=0, tiled=True),
        lax.all_gather(query_weight, "dp", axis=0, tiled=True),
        lax.all_gather(key_weight, "dp", axis=0, tiled=True),
        lax.all_gather(value_weight, "dp", axis=0, tiled=True),
        lax.all_gather(output_weight, "dp", axis=0, tiled=True),
    )
    gain_two, w_gate, w_up, w_down = (
        lax.all_gather(second_gain, "dp", axis=0, tiled=True),
        lax.all_gather(gate_weight, "dp", axis=0, tiled=True),
        lax.all_gather(up_weight, "dp", axis=0, tiled=True),
        lax.all_gather(down_weight, "dp", axis=0, tiled=True),
    )
    gain_one_f = gain_one.astype(jnp.float32)
    gain_two_f = gain_two.astype(jnp.float32)
    grad_rows = out_grad.reshape(rows, width)
    grad_down = product(hidden.T, grad_rows)
    grad_hidden = product(grad_rows, w_down.T)
    unused, gate_back = jax.vjp(gated, gate, upper)
    grad_gate, grad_upper = gate_back(grad_hidden)
    grad_gate = grad_gate.astype(jnp.bfloat16)
    grad_upper = grad_upper.astype(jnp.bfloat16)
    grad_wgate = product(normal_two.T, grad_gate)
    grad_wup = product(normal_two.T, grad_upper)
    grad_normal_two = product(grad_gate, w_gate.T) + product(grad_upper, w_up.T)
    unused_two, norm_back_two = jax.vjp(normed, middle, gain_two_f)
    grad_middle, grad_gain_two = norm_back_two(grad_normal_two)
    grad_middle = grad_middle + grad_rows.astype(jnp.float32)
    ffn_terms = (
        lax.psum_scatter(
            grad_gain_two.astype(jnp.bfloat16), "dp", scatter_dimension=0, tiled=True
        ).astype(jnp.float32),
        lax.psum_scatter(
            grad_wgate.astype(jnp.bfloat16), "dp", scatter_dimension=0, tiled=True
        ).astype(jnp.float32),
        lax.psum_scatter(
            grad_wup.astype(jnp.bfloat16), "dp", scatter_dimension=0, tiled=True
        ).astype(jnp.float32),
        lax.psum_scatter(
            grad_down.astype(jnp.bfloat16), "dp", scatter_dimension=0, tiled=True
        ).astype(jnp.float32),
    )
    ffn_total = (
        lax.psum(ffn_terms[0].astype(jnp.bfloat16), "ctx").astype(jnp.float32),
        lax.psum(ffn_terms[1].astype(jnp.bfloat16), "ctx").astype(jnp.float32),
        lax.psum(ffn_terms[2].astype(jnp.bfloat16), "ctx").astype(jnp.float32),
        lax.psum(ffn_terms[3].astype(jnp.bfloat16), "ctx").astype(jnp.float32),
    )
    grad_branch = grad_middle.astype(jnp.bfloat16)
    grad_woutput = product(mixed_rows.T, grad_branch)
    grad_mixed = product(grad_branch, w_output.T).astype(jnp.bfloat16)
    grad_query, grad_keys_all, grad_values_all = lax.map(
        attend_back, (shaped(query), keys_all, values_all, shaped(grad_mixed), logsum)
    )
    grad_keys, grad_values = (
        lax.psum_scatter(
            grad_keys_all.astype(jnp.bfloat16), "ctx", scatter_dimension=1, tiled=True
        ).astype(jnp.float32),
        lax.psum_scatter(
            grad_values_all.astype(jnp.bfloat16), "ctx", scatter_dimension=1, tiled=True
        ).astype(jnp.float32),
    )
    grad_keys = grad_keys.astype(jnp.bfloat16)
    grad_values = grad_values.astype(jnp.bfloat16)
    grad_query = grad_query.reshape(rows, width)
    grad_keys = grad_keys.reshape(rows, width)
    grad_values = grad_values.reshape(rows, width)
    grad_wquery = product(normal_one.T, grad_query)
    grad_wkey = product(normal_one.T, grad_keys)
    grad_wvalue = product(normal_one.T, grad_values)
    grad_normal_one = (
        product(grad_query, w_query.T)
        + product(grad_keys, w_key.T)
        + product(grad_values, w_value.T)
    )
    unused_one, norm_back_one = jax.vjp(normed, inputs, gain_one_f)
    grad_inputs, grad_gain_one = norm_back_one(grad_normal_one)
    in_grad = (grad_inputs + grad_middle).astype(jnp.bfloat16).reshape(seqs, local, width)
    attn_terms = (
        lax.psum_scatter(
            grad_gain_one.astype(jnp.bfloat16), "dp", scatter_dimension=0, tiled=True
        ).astype(jnp.float32),
        lax.psum_scatter(
            grad_wquery.astype(jnp.bfloat16), "dp", scatter_dimension=0, tiled=True
        ).astype(jnp.float32),
        lax.psum_scatter(
            grad_wkey.astype(jnp.bfloat16), "dp", scatter_dimension=0, tiled=True
        ).astype(jnp.float32),
        lax.psum_scatter(
            grad_wvalue.astype(jnp.bfloat16), "dp", scatter_dimension=0, tiled=True
        ).astype(jnp.float32),
        lax.psum_scatter(
            grad_woutput.astype(jnp.bfloat16), "dp", scatter_dimension=0, tiled=True
        ).astype(jnp.float32),
    )
    attn_total = (
        lax.psum(attn_terms[0].astype(jnp.bfloat16), "ctx").astype(jnp.float32),
        lax.psum(attn_terms[1].astype(jnp.bfloat16), "ctx").astype(jnp.float32),
        lax.psum(attn_terms[2].astype(jnp.bfloat16), "ctx").astype(jnp.float32),
        lax.psum(attn_terms[3].astype(jnp.bfloat16), "ctx").astype(jnp.float32),
        lax.psum(attn_terms[4].astype(jnp.bfloat16), "ctx").astype(jnp.float32),
    )
    return (
        layer_out,
        in_grad,
        attn_total[0],
        attn_total[1],
        attn_total[2],
        attn_total[3],
        attn_total[4],
        ffn_total[0],
        ffn_total[1],
        ffn_total[2],
        ffn_total[3],
    )


def solution(mesh):
    in_specs = (
        P("dp", "ctx", None),
        P("dp", "ctx", None),
        P("dp"),
        P("dp", None),
        P("dp", None),
        P("dp", None),
        P("dp", None),
        P("dp"),
        P("dp", None),
        P("dp", None),
        P("dp", None),
    )
    out_specs = (
        P("dp", "ctx", None),
        P("dp", "ctx", None),
        P("dp"),
        P("dp", None),
        P("dp", None),
        P("dp", None),
        P("dp", None),
        P("dp"),
        P("dp", None),
        P("dp", None),
        P("dp", None),
    )
    return jax.shard_map(
        on_device, mesh=mesh, in_specs=in_specs, out_specs=out_specs, check_vma=False
    )
```

profile of v0, /device:TPU:0, one launch (start us, length us, event | category | flops | bytes accessed | tf_op | source)
XLA Modules:
  0.0 1049.3 jit_solution(17920821551046934564)
XLA Ops:
  8.0 0.7 all-gather.14.cloned.1.call-update
  10.1 1.9 all-gather.2
  12.1 1.2 fusion.29
  13.8 7.7 all-gather.18.cloned.1.call-done
  21.5 2.7 convolution_convert_fusion.8
  24.3 9.2 all-gather.14.cloned.1.call-done
  33.5 2.5 convolution_convert_fusion.10
  36.7 0.7 all-gather.22.cloned.1.call-update
  37.4 0.7 all-gather.24.cloned.1.call-update
  38.9 1.8 all-gather.3
  40.8 4.7 all-gather.16.cloned.1.call-done
  45.5 1.8 convolution_convert_fusion.9
  47.5 96.6 %all-gather.30.cloned.1.call-done = bf16[4096,768]{1,0:T(8,128)(2,1)} async-done(((bf16[256,768]{1,0:T(8,128)(2,1)}), bf16[4096,768]{1,0:T(8,128)(2,1)}) %all-gather.30.cloned.1.call-update) | async-done | bytes 6291472 | tf_op jit(solution)/shard_map/all_gather | solution.py:115
  144.0 8.7 copy.36
  152.7 22.9 %multiply_reduce_fusion.1 = (f32[12,256]{1,0:T(8,128)S(1)}, f32[12,256,4096]{2,1,0:T(8,128)}) fusion(bf16[256,12,64]{0,2,1:T(8,128)(2,1)S(1)} %bitcast.127, bf16[4096,12,64]{0,2,1:T(8,128)(2,1)} %bitcast.119), kind=kOutput, calls=%fused_computation.6 | convolution fusion | flops 1635775488 | bytes 57028608 | tf_op jit(solution)/shard_map/while/body/eval_jaxpr/qhd,khd->hqk/dot_general | solution.py:24
  175.7 20.5 %fusion = f32[12,256]{1,0:T(8,128)S(1)} fusion(f32[12,256,4096]{2,1,0:T(8,128)} %get-tuple-element.75, f32[12,256]{1,0:T(8,128)S(1)} %get-tuple-element.74), kind=kLoop, calls=%fused_computation.5 | loop fusion | flops 37745664 | bytes 50356224 | tf_op jit(solution)/shard_map/while/body/eval_jaxpr/reduce_sum | solution.py:34
  196.2 43.5 %all-gather.28.cloned.1.call-done = bf16[4096,768]{1,0:T(8,128)(2,1)} async-done(((bf16[256,768]{1,0:T(8,128)(2,1)}), bf16[4096,768]{1,0:T(8,128)(2,1)}) %all-gather.28.cloned.1.call-update) | async-done | bytes 6291472 | tf_op jit(solution)/shard_map/all_gather | solution.py:116
  239.7 8.7 copy.34
  248.4 22.0 %fusion.19 = bf16[12,64,256]{2,1,0:T(8,128)(2,1)S(1)} fusion(bf16[4096,12,64]{0,2,1:T(8,128)(2,1)} %bitcast.121, f32[12,256,4096]{2,1,0:T(8,128)} %get-tuple-element.75, f32[12,256]{1,0:T(8,128)S(1)} %fusion, f32[12,256]{1,0:T(8,128)S(1)} %get-tuple-element.74), kind=kOutput, calls=%fused_computation.45 | convolution fusion | flops 1661140992 | bytes 57040896 | tf_op jit(solution)/shard_map/while/body/eval_jaxpr/hqk,khd->qhd/dot_general | solution.py:36
  270.5 1.9 multiply_reduce_fusion.4
  272.6 4.6 fusion.57
  277.2 1.3 all-gather.24.cloned.1.call-done
  278.5 4.2 fusion.58
  282.7 10.7 %all-gather.26.cloned.1.call-done = bf16[2048,768]{1,0:T(8,128)(2,1)} async-done(((bf16[1024,768]{1,0:T(8,128)(2,1)}), bf16[2048,768]{1,0:T(8,128)(2,1)}) %all-gather.26.cloned.1.call-update) | async-done | bytes 3145744 | tf_op jit(solution)/shard_map/all_gather | solution.py:125
  293.3 6.9 multiply_convert_fusion.2
  300.3 1.0 fusion.59
  301.3 1.6 copy-done.1
  302.9 1.7 multiply_reduce_fusion.2
  305.6 35.5 %multiply_reduce_fusion = (f32[12,256]{1,0:T(8,128)}, f32[12,256,4096]{2,1,0:T(8,128)}) fusion(f32[12,256,4096]{2,1,0:T(8,128)} %get-tuple-element.75, f32[12,256]{1,0:T(8,128)S(1)} %log_add_fusion, bf16[256,12,64]{0,2,1:T(8,128)(2,1)S(1)} %bitcast.125, bf16[4096,12,64]{0,2,1:T(8,128)(2,1)} %bitcast.122), kind=kOutput, calls=%fused_computation.1 | convolution fusion | flops 1660941312 | bytes 107372544 | tf_op jit(solution)/shard_map/while/body/eval_jaxpr/qhd,khd->hqk/dot_general | solution.py:43
  341.1 40.2 %multiply_convert_fusion = bf16[12,256,4096]{2,1,0:T(8,128)(2,1)} fusion(f32[12,256,4096]{2,1,0:T(8,128)} %get-tuple-element.80, f32[12,256,4096]{2,1,0:T(8,128)} %get-tuple-element.75, f32[12,256]{1,0:T(8,128)} %get-tuple-element.79, f32[12,256]{1,0:T(8,128)S(1)} %log_add_fusion), kind=kLoop, calls=%fused_computation | loop fusion | flops 62914560 | bytes 125853696 | tf_op jit(solution)/shard_map/while/body/eval_jaxpr/convert_element_type | solution.py:47
  381.3 15.2 %multiply_convert_fusion.1 = bf16[12,64,4096]{2,1,0:T(8,128)(2,1)} fusion(bf16[256,12,64]{0,2,1:T(8,128)(2,1)S(1)} %bitcast.128, bf16[12,256,4096]{2,1,0:T(8,128)(2,1)} %multiply_convert_fusion), kind=kOutput, calls=%fused_computation.12 | convolution fusion | flops 1616904192 | bytes 31850496 | tf_op jit(solution)/shard_map/while/body/eval_jaxpr/hqk,qhd->khd/dot_general | solution.py:62
  396.6 22.0 %fusion.7 = bf16[12,64,4096]{2,1,0:T(8,128)(2,1)} fusion(bf16[256,12,64]{0,2,1:T(8,128)(2,1)S(1)} %bitcast.126, f32[12,256,4096]{2,1,0:T(8,128)} %get-tuple-element.75, f32[12,256]{1,0:T(8,128)S(1)} %log_add_fusion), kind=kOutput, calls=%fused_computation.13 | convolution fusion | flops 1651507200 | bytes 57028608 | tf_op jit(solution)/shard_map/while/body/eval_jaxpr/hqk,qhd->khd/dot_general | solution.py:65
  418.6 14.4 %fusion.18 = bf16[12,64,256]{2,1,0:T(8,128)(2,1)S(1)} fusion(bf16[4096,12,64]{0,2,1:T(8,128)(2,1)} %bitcast.120, bf16[12,256,4096]{2,1,0:T(8,128)(2,1)} %multiply_convert_fusion), kind=kOutput, calls=%fused_computation.44 | convolution fusion | flops 1611005952 | bytes 31850496 | tf_op jit(solution)/shard_map/while/body/eval_jaxpr/hqk,khd->qhd/dot_general | solution.py:52
  433.1 1.6 convolution_convert_fusion.6
  434.8 1.5 convolution_convert_fusion.3
  436.4 3.9 convolution_convert_fusion.2
  440.4 1.2 copy-done.6
  441.5 2.7 convolution_convert_fusion.1
  444.3 1.2 copy-done.9
  445.6 2.7 convolution_convert_fusion
  448.3 95.9 %reduce-scatter.10.cloned.1.call-done = bf16[1,256,768]{1,2,0:T(8,128)(2,1)} async-done(((bf16[1,4096,768]{1,2,0:T(8,128)(2,1)}), bf16[1,256,768]{1,2,0:T(8,128)(2,1)}) %reduce-scatter.10.cloned.1.call-update) | async-done | bytes 393232 | tf_op jit(solution)/shard_map/reduce_scatter | solution.py:189
  544.2 2.6 convolution_convert_fusion.5
  546.9 148.6 %reduce-scatter.12.cloned.1.call-done = bf16[1,256,768]{1,2,0:T(8,128)(2,1)} async-done(((bf16[1,4096,768]{1,2,0:T(8,128)(2,1)}), bf16[1,256,768]{1,2,0:T(8,128)(2,1)}) %reduce-scatter.12.cloned.1.call-update) | async-done | bytes 393232 | tf_op jit(solution)/shard_map/reduce_scatter | solution.py:192
  695.5 2.6 convolution_convert_fusion.4
  698.4 7.6 reduce-scatter.14.cloned.1.call-done
  706.0 12.8 %reduce-scatter.20.cloned.1.call-done = bf16[384,768]{1,0:T(8,128)(2,1)} async-done(((bf16[768,768]{1,0:T(8,128)(2,1)}), bf16[384,768]{1,0:T(8,128)(2,1)}) %reduce-scatter.20.cloned.1.call-update) | async-done | bytes 589840 | tf_op jit(solution)/shard_map/reduce_scatter | solution.py:225
  718.8 14.8 %reduce-scatter.22.cloned.1.call-done = bf16[384,2048]{1,0:T(8,128)(2,1)} async-done(((bf16[768,2048]{1,0:T(8,128)(2,1)}), bf16[384,2048]{1,0:T(8,128)(2,1)}) %reduce-scatter.22.cloned.1.call-update) | async-done | bytes 1572880 | tf_op jit(solution)/shard_map/reduce_scatter | solution.py:166
  733.6 14.9 %reduce-scatter.24.cloned.1.call-done = bf16[384,2048]{1,0:T(8,128)(2,1)} async-done(((bf16[768,2048]{1,0:T(8,128)(2,1)}), bf16[384,2048]{1,0:T(8,128)(2,1)}) %reduce-scatter.24.cloned.1.call-update) | async-done | bytes 1572880 | tf_op jit(solution)/shard_map/reduce_scatter | solution.py:169
  748.4 14.8 %reduce-scatter.26.cloned.1.call-done = bf16[1024,768]{1,0:T(8,128)(2,1)} async-done(((bf16[2048,768]{1,0:T(8,128)(2,1)}), bf16[1024,768]{1,0:T(8,128)(2,1)}) %reduce-scatter.26.cloned.1.call-update) | async-done | bytes 1572880 | tf_op jit(solution)/shard_map/reduce_scatter | solution.py:172
  763.2 12.6 %reduce-scatter.16.cloned.1.call-done = bf16[384,768]{1,0:T(8,128)(2,1)} async-done(((bf16[768,768]{1,0:T(8,128)(2,1)}), bf16[384,768]{1,0:T(8,128)(2,1)}) %reduce-scatter.16.cloned.1.call-update) | async-done | bytes 589840 | tf_op jit(solution)/shard_map/reduce_scatter | solution.py:219
  775.8 12.6 %reduce-scatter.18.cloned.1.call-done = bf16[384,768]{1,0:T(8,128)(2,1)} async-done(((bf16[768,768]{1,0:T(8,128)(2,1)}), bf16[384,768]{1,0:T(8,128)(2,1)}) %reduce-scatter.18.cloned.1.call-update) | async-done | bytes 589840 | tf_op jit(solution)/shard_map/reduce_scatter | solution.py:222
  790.3 1.8 fusion.60
  792.1 3.8 fusion.20
  797.1 2.5 all-reduce.4
  799.8 43.9 %all-reduce.2 = (bf16[384]{0:T(512)(128)(2,1)S(1)}, bf16[384]{0:T(512)(128)(2,1)S(1)}) all-reduce(bf16[384]{0:T(512)(128)(2,1)S(1)} %dynamic-slice.3, bf16[384]{0:T(512)(128)(2,1)S(1)} %dynamic-slice.5), channel_id=1, replica_groups=mesh['dp'=2,'ctx'=16] {'ctx'}, use_global_device_ids=true, to_apply=%region_11.12 | all-reduce | flops 768 | bytes 3072 | tf_op jit(solution)/shard_map/psum | solution.py:230
  844.9 1.0 fusion.36
  845.9 184.0 %all-reduce.7.cloned.1.call-done = (bf16[384,768]{1,0:T(8,128)(2,1)}, bf16[384,768]{1,0:T(8,128)(2,1)}, bf16[384,768]{1,0:T(8,128)(2,1)}, bf16[384,768]{1,0:T(8,...) async-done(((bf16[384,768]{1,0:T(8,128)(2,1)}, bf16[384,768]{1,0:T(8,128)(2,1)}, bf16[384,768]{1,0:T(8,128)(2,1)}, ...) | async-done | bytes 7077904 | tf_op jit(solution)/shard_map/psum | solution.py:231
  1029.9 2.3 convert_element_type.247
  1032.2 2.2 convert_element_type.249
  1034.3 1.1 convert_element_type.251
  1035.4 1.1 convert_element_type.253
  1036.5 2.0 convert_element_type.257
  1038.6 2.0 convert_element_type.259
  1040.6 1.9 convert_element_type.261
  (121 shorter events, 10.3 us)
Async XLA Ops:
  7.2 26.3 %copy-start = (bf16[1,256,768]{2,1,0:T(8,128)(2,1)S(1)}, bf16[1,256,768]{2,1,0:T(8,128)(2,1)}, u32[]{:S(2)}) copy-start(bf16[1,256,768]{2,1,0:T(8,128)(2,1)} %param.11) | copy-start | bytes 1179652
  7.2 14.3 %all-gather.18.cloned.1.call-start = ((), (), s32[]{:S(2)}) async-start(), calls=%async_computation.11 | async-start | bytes 1769472 | tf_op jit(solution)/shard_map/all_gather | solution.py:104
  7.9 25.6 %all-gather.14.cloned.1.call-start = ((), (), s32[]{:S(2)}) async-start(), calls=%async_computation.9 | async-start | bytes 1769472 | tf_op jit(solution)/shard_map/all_gather | solution.py:105
  8.7 36.8 %all-gather.16.cloned.1.call-start = ((), (), s32[]{:S(2)}) async-start(), calls=%async_computation.10 | async-start | bytes 1769472 | tf_op jit(solution)/shard_map/all_gather | solution.py:103
  9.4 134.6 %all-gather.30.cloned.1.call-start = ((), (), s32[]{:S(2)}) async-start(), calls=%async_computation.26 | async-start | bytes 6684672 | tf_op jit(solution)/shard_map/all_gather | solution.py:115
  12.1 33.4 %copy-start.23 = (f32[768]{0:T(1024)}, f32[768]{0:T(1024)S(1)}, u32[]{:S(2)}) copy-start(f32[768]{0:T(1024)S(1)} %reshape.240) | copy-start | bytes 9220
  13.2 0.6 copy-start.27
  13.8 31.6 %copy-start.25 = (f32[256]{0:T(256)}, f32[256]{0:T(256)S(1)}, u32[]{:S(2)}) copy-start(f32[256]{0:T(256)S(1)} %fusion.47) | copy-start | bytes 3076
  24.2 215.5 %all-gather.28.cloned.1.call-start = ((), (), s32[]{:S(2)}) async-start(), calls=%async_computation.25 | async-start | bytes 6684672 | tf_op jit(solution)/shard_map/all_gather | solution.py:116
  36.0 2.9 copy-start.30
  36.1 234.4 %all-gather.20.cloned.1.call-start = ((), (), s32[]{:S(2)}) async-start(), calls=%async_computation.12 | async-start | bytes 1769472 | tf_op jit(solution)/shard_map/all_gather | solution.py:106
  36.6 235.9 %all-gather.22.cloned.1.call-start = ((), (), s32[]{:S(2)}) async-start(), calls=%async_computation.13 | async-start | bytes 4718592 | tf_op jit(solution)/shard_map/all_gather | solution.py:123
  37.4 241.1 %all-gather.24.cloned.1.call-start = ((), (), s32[]{:S(2)}) async-start(), calls=%async_computation.14 | async-start | bytes 4718592 | tf_op jit(solution)/shard_map/all_gather | solution.py:124
  38.1 255.2 %all-gather.26.cloned.1.call-start = ((), (), s32[]{:S(2)}) async-start(), calls=%async_computation.15 | async-start | bytes 4718592 | tf_op jit(solution)/shard_map/all_gather | solution.py:125
  38.9 505.3 %reduce-scatter.10.cloned.1.call-start = ((), (), s32[]{:S(2)}) async-start(), calls=%async_computation.16 | async-start | bytes 6684672 | tf_op jit(solution)/shard_map/reduce_scatter | solution.py:189
  47.4 105.3 %copy-start.3 = (bf16[256,768]{0,1:T(8,128)(2,1)}, bf16[256,768]{0,1:T(8,128)(2,1)S(1)}, u32[]{:S(2)}) copy-start(bf16[256,768]{0,1:T(8,128)(2,1)S(1)} %copy.35) | copy-start | bytes 1179652
  277.2 16.1 %copy-start.11 = (bf16[1,256,768]{2,1,0:T(8,128)(2,1)S(1)}, bf16[1,256,768]{2,1,0:T(8,128)(2,1)}, u32[]{:S(2)}) copy-start(bf16[1,256,768]{2,1,0:T(8,128)(2,1)} %param.12) | copy-start | bytes 1179652
  293.3 7.0 copy-start.10
  300.3 4.4 copy-start.5
  300.3 4.4 copy-start.20
  300.3 2.6 copy-start.1
  302.9 2.0 copy-start.2
  341.1 40.2 %copy-start.4 = (bf16[256,768]{0,1:T(8,128)(2,1)S(1)}, bf16[256,768]{0,1:T(8,128)(2,1)}, u32[]{:S(2)}) copy-start(bf16[256,768]{0,1:T(8,128)(2,1)} %copy-done.3) | copy-start | bytes 1179652
  396.5 299.0 %reduce-scatter.12.cloned.1.call-start = ((), (), s32[]{:S(2)}) async-start(), calls=%async_computation.17 | async-start | bytes 6684672 | tf_op jit(solution)/shard_map/reduce_scatter | solution.py:192
  418.6 14.5 %copy-start.24 = (f32[768]{0:T(1024)S(1)}, f32[768]{0:T(1024)}, u32[]{:S(2)}) copy-start(f32[768]{0:T(1024)} %copy-done.23) | copy-start | bytes 9220
  418.6 14.5 %copy-start.26 = (f32[256]{0:T(256)S(1)}, f32[256]{0:T(256)}, u32[]{:S(2)}) copy-start(f32[256]{0:T(256)} %copy-done.25) | copy-start | bytes 3076
  418.6 287.4 %reduce-scatter.14.cloned.1.call-start = ((), (), s32[]{:S(2)}) async-start(), calls=%async_computation.18 | async-start | bytes 1769472 | tf_op jit(solution)/shard_map/reduce_scatter | solution.py:216
  433.1 3.2 copy-start.7
  434.7 284.0 %reduce-scatter.20.cloned.1.call-start = ((), (), s32[]{:S(2)}) async-start(), calls=%async_computation.21 | async-start | bytes 1769472 | tf_op jit(solution)/shard_map/reduce_scatter | solution.py:225
  436.3 297.2 %reduce-scatter.22.cloned.1.call-start = ((), (), s32[]{:S(2)}) async-start(), calls=%async_computation.22 | async-start | bytes 4718592 | tf_op jit(solution)/shard_map/reduce_scatter | solution.py:166
  440.3 1.2 copy-start.6
  440.3 308.1 %reduce-scatter.24.cloned.1.call-start = ((), (), s32[]{:S(2)}) async-start(), calls=%async_computation.23 | async-start | bytes 4718592 | tf_op jit(solution)/shard_map/reduce_scatter | solution.py:169
  444.2 1.3 copy-start.9
  444.2 1.4 copy-start.12
  444.2 318.9 %reduce-scatter.26.cloned.1.call-start = ((), (), s32[]{:S(2)}) async-start(), calls=%async_computation.24 | async-start | bytes 4718592 | tf_op jit(solution)/shard_map/reduce_scatter | solution.py:172
  448.3 327.5 %reduce-scatter.16.cloned.1.call-start = ((), (), s32[]{:S(2)}) async-start(), calls=%async_computation.19 | async-start | bytes 1769472 | tf_op jit(solution)/shard_map/reduce_scatter | solution.py:219
  546.8 241.5 %reduce-scatter.18.cloned.1.call-start = ((), (), s32[]{:S(2)}) async-start(), calls=%async_computation.20 | async-start | bytes 1769472 | tf_op jit(solution)/shard_map/reduce_scatter | solution.py:222
  698.1 331.8 %all-reduce.7.cloned.1.call-start = ((), (), s32[]{:S(2)}) async-start(), calls=%async_computation.27 | async-start | bytes 14155776 | tf_op jit(solution)/shard_map/psum | solution.py:231
  788.4 0.7 copy-start.31
  788.4 1.9 copy-start.8
  792.1 3.8 copy-start.13
  792.1 3.8 copy-start.18
  792.1 4.3 copy-start.14
  792.1 4.3 copy-start.19
  795.9 1.3 copy-start.29
  795.9 49.0 %copy-start.28 = (f32[256]{0:T(256)S(1)}, f32[256]{0:T(256)}, u32[]{:S(2)}) copy-start(f32[256]{0:T(256)} %copy-done.27) | copy-start | bytes 3076
  1029.9 4.5 copy-start.22
  1029.9 5.6 copy-start.21
  1029.9 6.7 copy-start.17
  1035.4 3.1 copy-start.16
  1038.6 2.0 copy-start.15
Sparse Core Ops, SparseCore 0:
  9.6 11.9 all-gather.17
  23.1 10.3 all-gather.13
  35.0 10.3 all-gather.15
  48.7 95.2 all-gather.29
  147.2 92.4 all-gather.27
  241.1 7.4 all-gather.19
  250.2 13.2 all-gather.21
  265.0 13.3 all-gather.23
  280.0 13.2 all-gather.25
  396.6 147.5 reduce-scatter.9
  549.4 146.0 reduce-scatter.11
  698.1 7.7 reduce-scatter.13
  708.9 9.8 reduce-scatter.19
  721.4 12.0 reduce-scatter.21
  736.3 12.0 reduce-scatter.23
  751.1 12.0 reduce-scatter.25
  765.9 9.8 reduce-scatter.15
  778.5 9.8 reduce-scatter.17
  795.9 233.8 all-reduce.6
where the time goes:
time: 1060 us; the launch traced here: 1050 us
  waiting for transfers between devices  697 us (66%)
  matrix products  184 us (17%)
  other arithmetic  77.1 us (7%)
  blocking collectives  50.1 us (5%)
  local copies, waits for them, and re-layouts  24.6 us (2%)
  between operations  15.3 us (1%)
    psum x1, waiting for transfers between devices, on_device(): lax.psum(attn_terms[1].astype(jnp.bfloat16), 'ctx').astype(jnp.float32)  184 us
    reduce_scatter x1, waiting for transfers between devices, on_device(): lax.psum_scatter(grad_values_all.astype(jnp.bfloat16), 'ctx', scatter_dim...  149 us
    all_gather x1, waiting for transfers between devices, on_device(): lax.all_gather(shaped(keys), 'ctx', axis=1, tiled=True)  96.6 us
    reduce_scatter x1, waiting for transfers between devices, on_device(): lax.psum_scatter(grad_keys_all.astype(jnp.bfloat16), 'ctx', scatter_dimen...  95.9 us
    dot_general x21, matrix products, product(): return jnp.dot(left, right, preferred_element_type=jnp.float32)  52.2 us
    psum x1, blocking collectives, on_device(): lax.psum(attn_terms[0].astype(jnp.bfloat16), 'ctx').astype(jnp.float32)  43.9 us
    all_gather x1, waiting for transfers between devices, on_device(): lax.all_gather(shaped(values), 'ctx', axis=1, tiled=True)  43.5 us
    convert_element_type x1, other arithmetic, back_core(): grad_score = (probs * (grad_prob - delta[..., None])).astype(jnp.bfloat16)  40.2 us
  transfers between devices with their start and end apart: 19, of which 17 were waited for; matrix products, arithmetic and copies ran while one was open for 16% of the time, Pallas kernels for 0%

commit v1 on v0

--- a/solution.py
+++ b/solution.py
@@ -6,6 +6,13 @@
 HEADS = 12
 HEAD_DIM = 64
 EPS = 1e-06
+
+
+def edge_make(q_in, dimension_no):
+    f_next = list(q_in.shape[1:])
+    f_next[dimension_no] *= q_in.shape[0]
+    n_now = jnp.moveaxis(q_in, 0, dimension_no).reshape(f_next)
+    return n_now
 
 
 def normed(rows, gain):
@@ -111,9 +118,34 @@
     query = product(normal_one, w_query).astype(jnp.bfloat16)
     keys = product(normal_one, w_key).astype(jnp.bfloat16)
     values = product(normal_one, w_value).astype(jnp.bfloat16)
+
+    def cubes_link(slab_in, mesh_dim, axis_no):
+        p_count = lax.psum(1, axis_name=mesh_dim)
+        gallery = tuple(((k, (k + 1) % p_count) for k in range(p_count)))
+        pool = tuple(((it, p) for p, it in gallery))
+        finding, v_next = ([], [])
+        for hop_no in tuple(range(p_count - 1)):
+            if hop_no % 2 == 0:
+                tall = lax.ppermute(
+                    finding[-1] if finding else slab_in, axis_name=mesh_dim, perm=gallery
+                )
+                finding.append(tall)
+            else:
+                near = lax.ppermute(
+                    v_next[-1] if v_next else slab_in, axis_name=mesh_dim, perm=pool
+                )
+                v_next.append(near)
+        g_now = jnp.stack([*finding[::-1], slab_in, *v_next])
+        res = lax.axis_index(mesh_dim)
+        side_arr = len(finding)
+        piece_out = res - side_arr
+        g_now = g_now[(jnp.arange(p_count) - piece_out) % p_count]
+        t1 = edge_make(g_now, axis_no)
+        return t1
+
     keys_all, values_all = (
         lax.all_gather(shaped(keys), "ctx", axis=1, tiled=True),
-        lax.all_gather(shaped(values), "ctx", axis=1, tiled=True),
+        cubes_link(shaped(values), "ctx", 1),
     )
     mixed, logsum = lax.map(attend, (shaped(query), keys_all, values_all))
     mixed_rows = mixed.reshape(rows, width)

time: 1060 us -> 1090 us (1.028)
  starting transfers between devices: 0.98 us -> 85.3 us
  waiting for transfers between devices: 697 us -> 617 us
  local copies, waits for them, and re-layouts: 24.6 us -> 58.2 us
    all_gather x1, waiting for transfers between devices: 96.6 us -> 0.01 us  [on_device(): lax.all_gather(shaped(keys), 'ctx', axis=1, tiled=True)]
    ppermute x0 -> x15, starting transfers between devices: none -> 84.4 us  [the longest x7 64.1 us: cubes_link(): lax.ppermute(v_next[-1] if v_next else slab_in, axis_name=mesh_dim, perm=...]
    ppermute x0 -> x15, waiting for transfers between devices: none -> 82.8 us  [the longest x8 73.8 us: cubes_link(): lax.ppermute(finding[-1] if finding else slab_in, axis_name=mesh_dim, per...]
    all_gather x1 -> x0, waiting for transfers between devices: 43.5 us -> none  [on_device(): lax.all_gather(shaped(values), 'ctx', axis=1, tiled=True)]
    gather x0 -> x2, local copies, waits for them, and re-layouts: none -> 15.9 us  [cubes_link(): g_now = g_now[(jnp.arange(p_count) - piece_out) % p_count]]
    unnamed x69 -> x86, local copies, waits for them, and re-layouts: 6.81 us -> 21 us
  transfers between devices with their start and end apart: 19 -> 33, of which waited for: 17 -> 23; matrix products, arithmetic and copies ran while one was open for 16% -> 19% of each run, Pallas kernels for 0% -> 0%
where the time goes in v1:
time: 1090 us
  waiting for transfers between devices  617 us (57%)
  matrix products  182 us (17%)
  starting transfers between devices  85.3 us (8%)
  other arithmetic  80.7 us (7%)
  local copies, waits for them, and re-layouts  58.2 us (5%)
  blocking collectives  50.1 us (5%)
  between operations  15.7 us (1%)
    psum x1, waiting for transfers between devices, on_device(): lax.psum(attn_terms[1].astype(jnp.bfloat16), 'ctx').astype(jnp.float32)  184 us
    reduce_scatter x1, waiting for transfers between devices, on_device(): lax.psum_scatter(grad_values_all.astype(jnp.bfloat16), 'ctx', scatter_dim...  148 us
    reduce_scatter x1, waiting for transfers between devices, on_device(): lax.psum_scatter(grad_keys_all.astype(jnp.bfloat16), 'ctx', scatter_dimen...  92.5 us
    ppermute x8, waiting for transfers between devices, cubes_link(): lax.ppermute(finding[-1] if finding else slab_in, axis_name=mesh_dim, per...  73.8 us
    ppermute x7, starting transfers between devices, cubes_link(): lax.ppermute(v_next[-1] if v_next else slab_in, axis_name=mesh_dim, perm=...  64.1 us
    dot_general x21, matrix products, product(): return jnp.dot(left, right, preferred_element_type=jnp.float32)  53.5 us
    psum x1, blocking collectives, on_device(): lax.psum(attn_terms[0].astype(jnp.bfloat16), 'ctx').astype(jnp.float32)  44 us
    convert_element_type x1, other arithmetic, back_core(): grad_score = (probs * (grad_prob - delta[..., None])).astype(jnp.bfloat16)  40.1 us
  transfers between devices with their start and end apart: 33, of which 23 were waited for; matrix products, arithmetic and copies ran while one was open for 19% of the time, Pallas kernels for 0%

profile of v1, /device:TPU:0, one launch (start us, length us, event | category | flops | bytes accessed | tf_op | source)
XLA Modules:
  0.0 1088.5 jit_solution(3382366581399136043)
XLA Ops:
  13.3 8.2 all-gather.16.cloned.1.call-done
  21.5 2.7 convolution_convert_fusion.8
  26.2 7.3 all-gather.12.cloned.1.call-done
  37.1 13.3 %collective-permute-done = bf16[1,256,768]{2,1,0:T(8,128)(2,1)S(1)} collective-permute-done((bf16[1,256,768]{2,1,0:T(8,128)(2,1)S(1)}, bf16[1,256,768]{2,1,0:T(8,128)(2,1)S(1)}, u32[]{:S(2)}, u32[]{:S(2)}) %collective-permute-start) | collective-permute-done | bytes 393248 | tf_op jit(solution)/shard_map/ppermute | solution.py:129
  50.3 5.6 collective-permute-start.8
  55.9 14.0 %collective-permute-done.1 = bf16[1,256,768]{2,1,0:T(8,128)(2,1)S(1)} collective-permute-done((bf16[1,256,768]{2,1,0:T(8,128)(2,1)S(1)}, bf16[1,256,768]{2,1,0:T(8,128)(2,1)S(1)}, u32[]{:S(2)}, u32[]{:S(2)}) %collective-permute-start.1) | collective-permute-done | bytes 393248 | tf_op jit(solution)/shard_map/ppermute | solution.py:129
  70.0 2.5 collective-permute-start.2
  72.4 16.4 %collective-permute-start.9 = (bf16[1,256,768]{2,1,0:T(8,128)(2,1)S(1)}, bf16[1,256,768]{2,1,0:T(8,128)(2,1)S(1)}, u32[]{:S(2)}, u32[]{:S(2)}) collective-permute-start(bf16[1,256,768]{2,1,0:T(8,128)(2,1)S(1)} %collective-permute-done.8), channel_id=1, source_target_pairs={{1,0},{2,1},{3,2},{4,3},{5,4},{6,5},{7,6},{8,7},{9,8},{10,9},{11,1... | collective-permute-start | bytes 1179656 | tf_op jit(solution)/shard_map/ppermute | solution.py:134
  88.8 10.9 collective-permute-done.2
  99.7 4.9 collective-permute-start.3
  104.5 11.4 %collective-permute-start.10 = (bf16[1,256,768]{2,1,0:T(8,128)(2,1)S(1)}, bf16[1,256,768]{2,1,0:T(8,128)(2,1)S(1)}, u32[]{:S(2)}, u32[]{:S(2)}) collective-permute-start(bf16[1,256,768]{2,1,0:T(8,128)(2,1)S(1)} %collective-permute-done.9), channel_id=1, source_target_pairs={{1,0},{2,1},{3,2},{4,3},{5,4},{6,5},{7,6},{8,7},{9,8},{10,9},{11,1... | collective-permute-start | bytes 1179656 | tf_op jit(solution)/shard_map/ppermute | solution.py:134
  116.6 2.5 collective-permute-start.4
  119.1 3.9 collective-permute-done.10
  122.9 6.5 collective-permute-start.11
  129.4 11.1 %collective-permute-done.4 = bf16[1,256,768]{2,1,0:T(8,128)(2,1)S(1)} collective-permute-done((bf16[1,256,768]{2,1,0:T(8,128)(2,1)S(1)}, bf16[1,256,768]{2,1,0:T(8,128)(2,1)S(1)}, u32[]{:S(2)}, u32[]{:S(2)}) %collective-permute-start.4) | collective-permute-done | bytes 393248 | tf_op jit(solution)/shard_map/ppermute | solution.py:129
  140.6 3.2 collective-permute-start.5
  143.7 2.5 collective-permute-done.11
  146.2 9.5 collective-permute-start.12
  155.7 11.5 %collective-permute-done.5 = bf16[1,256,768]{2,1,0:T(8,128)(2,1)} collective-permute-done((bf16[1,256,768]{2,1,0:T(8,128)(2,1)S(1)}, bf16[1,256,768]{2,1,0:T(8,128)(2,1)}, u32[]{:S(2)}, u32[]{:S(2)}) %collective-permute-start.5) | collective-permute-done | bytes 393248 | tf_op jit(solution)/shard_map/ppermute | solution.py:129
  167.2 3.1 collective-permute-start.6
  172.8 2.6 collective-permute-done.12
  175.5 8.5 collective-permute-start.13
  184.0 6.7 collective-permute-done.6
  190.7 2.4 collective-permute-start.7
  194.4 2.5 convolution_convert_fusion.9
  198.1 6.2 collective-permute-start.14
  204.3 5.6 collective-permute-done.7
  229.5 6.3 gather_fusion
  235.9 9.6 copy.34
  245.5 10.5 reshape.271
  256.0 8.6 copy.36
  264.6 22.2 %multiply_reduce_fusion.1 = (f32[12,256]{1,0:T(8,128)S(1)}, f32[12,256,4096]{2,1,0:T(8,128)}) fusion(bf16[256,12,64]{0,2,1:T(8,128)(2,1)S(1)} %bitcast.162, bf16[4096,12,64]{0,2,1:T(8,128)(2,1)} %bitcast.156), kind=kOutput, calls=%fused_computation.7 | convolution fusion | flops 1635775488 | bytes 57028608 | tf_op jit(solution)/shard_map/while/body/eval_jaxpr/qhd,khd->hqk/dot_general | solution.py:31
  286.8 20.8 %fusion = f32[12,256]{1,0:T(8,128)S(1)} fusion(f32[12,256,4096]{2,1,0:T(8,128)} %get-tuple-element.75, f32[12,256]{1,0:T(8,128)S(1)} %get-tuple-element.74), kind=kLoop, calls=%fused_computation.6 | loop fusion | flops 37745664 | bytes 50356224 | tf_op jit(solution)/shard_map/while/body/eval_jaxpr/reduce_sum | solution.py:41
  307.6 19.2 %fusion.19 = bf16[12,64,256]{2,1,0:T(8,128)(2,1)S(1)} fusion(bf16[4096,12,64]{0,2,1:T(8,128)(2,1)S(1)} %copy-done, f32[12,256,4096]{2,1,0:T(8,128)} %get-tuple-element.75, f32[12,256]{1,0:T(8,128)S(1)} %fusion, f32[12,256]{1,0:T(8,128)S(1)} %get-tuple-element.74), kind=kOutput, calls=%fused_computation.46 | convolution fusion | flops 1661140992 | bytes 57040896 | tf_op jit(solution)/shard_map/while/body/eval_jaxpr/hqk,khd->qhd/dot_general | solution.py:43
  329.1 4.2 fusion.59
  333.3 4.2 fusion.60
  337.5 6.7 multiply_convert_fusion.2
  347.4 35.0 %multiply_reduce_fusion = (f32[12,256]{1,0:T(8,128)S(1)}, f32[12,256,4096]{2,1,0:T(8,128)}) fusion(f32[12,256,4096]{2,1,0:T(8,128)} %get-tuple-element.75, f32[12,256]{1,0:T(8,128)S(1)} %log_add_fusion, bf16[256,12,64]{0,2,1:T(8,128)(2,1)S(1)} %bitcast.160, bf16[4096,12,64]{0,2,1:T(8,128)(2,1)} %reshape.271), kind=kOutput, calls=%fused_computation.2 | convolution fusion | flops 1660941312 | bytes 107372544 | tf_op jit(solution)/shard_map/while/body/eval_jaxpr/qhd,khd->hqk/dot_general | solution.py:50
  382.4 40.1 %multiply_convert_fusion = bf16[12,256,4096]{2,1,0:T(8,128)(2,1)} fusion(f32[12,256,4096]{2,1,0:T(8,128)} %get-tuple-element.80, f32[12,256,4096]{2,1,0:T(8,128)} %get-tuple-element.75, f32[12,256]{1,0:T(8,128)S(1)} %get-tuple-element.79, f32[12,256]{1,0:T(8,128)S(1)} %log_add_fusion), kind=kLoop, calls=%fused_computation.1 | loop fusion | flops 62914560 | bytes 125853696 | tf_op jit(solution)/shard_map/while/body/eval_jaxpr/convert_element_type | solution.py:54
  422.4 15.2 %multiply_convert_fusion.1 = bf16[12,64,4096]{2,1,0:T(8,128)(2,1)} fusion(bf16[256,12,64]{0,2,1:T(8,128)(2,1)S(1)} %bitcast.163, bf16[12,256,4096]{2,1,0:T(8,128)(2,1)} %multiply_convert_fusion), kind=kOutput, calls=%fused_computation.13 | convolution fusion | flops 1616904192 | bytes 31850496 | tf_op jit(solution)/shard_map/while/body/eval_jaxpr/hqk,qhd->khd/dot_general | solution.py:69
  437.8 22.1 %fusion.7 = bf16[12,64,4096]{2,1,0:T(8,128)(2,1)} fusion(bf16[256,12,64]{0,2,1:T(8,128)(2,1)S(1)} %bitcast.161, f32[12,256,4096]{2,1,0:T(8,128)} %get-tuple-element.75, f32[12,256]{1,0:T(8,128)S(1)} %log_add_fusion), kind=kOutput, calls=%fused_computation.14 | convolution fusion | flops 1651507200 | bytes 57028608 | tf_op jit(solution)/shard_map/while/body/eval_jaxpr/hqk,qhd->khd/dot_general | solution.py:72
  460.0 14.4 %fusion.18 = bf16[12,64,256]{2,1,0:T(8,128)(2,1)S(1)} fusion(bf16[4096,12,64]{0,2,1:T(8,128)(2,1)} %bitcast.157, bf16[12,256,4096]{2,1,0:T(8,128)(2,1)} %multiply_convert_fusion), kind=kOutput, calls=%fused_computation.45 | convolution fusion | flops 1611005952 | bytes 31850496 | tf_op jit(solution)/shard_map/while/body/eval_jaxpr/hqk,khd->qhd/dot_general | solution.py:59
  476.1 2.6 convolution_convert_fusion.3
  478.8 3.9 convolution_convert_fusion.2
  482.8 2.7 convolution_convert_fusion.1
  485.5 4.0 convolution_convert_fusion
  489.6 92.5 %reduce-scatter.10.cloned.1.call-done = bf16[1,256,768]{1,2,0:T(8,128)(2,1)} async-done(((bf16[1,4096,768]{1,2,0:T(8,128)(2,1)}), bf16[1,256,768]{1,2,0:T(8,128)(2,1)}) %reduce-scatter.10.cloned.1.call-update) | async-done | bytes 393232 | tf_op jit(solution)/shard_map/reduce_scatter | solution.py:221
  582.2 2.6 convolution_convert_fusion.5
  584.9 147.5 %reduce-scatter.12.cloned.1.call-done = bf16[1,256,768]{1,2,0:T(8,128)(2,1)} async-done(((bf16[1,4096,768]{1,2,0:T(8,128)(2,1)}), bf16[1,256,768]{1,2,0:T(8,128)(2,1)}) %reduce-scatter.12.cloned.1.call-update) | async-done | bytes 393232 | tf_op jit(solution)/shard_map/reduce_scatter | solution.py:224
  732.4 2.6 convolution_convert_fusion.4
  735.3 7.7 reduce-scatter.14.cloned.1.call-done
  743.0 12.7 %reduce-scatter.20.cloned.1.call-done = bf16[384,768]{1,0:T(8,128)(2,1)} async-done(((bf16[768,768]{1,0:T(8,128)(2,1)}), bf16[384,768]{1,0:T(8,128)(2,1)}) %reduce-scatter.20.cloned.1.call-update) | async-done | bytes 589840 | tf_op jit(solution)/shard_map/reduce_scatter | solution.py:257
  755.7 14.9 %reduce-scatter.22.cloned.1.call-done = bf16[384,2048]{1,0:T(8,128)(2,1)} async-done(((bf16[768,2048]{1,0:T(8,128)(2,1)}), bf16[384,2048]{1,0:T(8,128)(2,1)}) %reduce-scatter.22.cloned.1.call-update) | async-done | bytes 1572880 | tf_op jit(solution)/shard_map/reduce_scatter | solution.py:198
  770.6 14.9 %reduce-scatter.24.cloned.1.call-done = bf16[384,2048]{1,0:T(8,128)(2,1)} async-done(((bf16[768,2048]{1,0:T(8,128)(2,1)}), bf16[384,2048]{1,0:T(8,128)(2,1)}) %reduce-scatter.24.cloned.1.call-update) | async-done | bytes 1572880 | tf_op jit(solution)/shard_map/reduce_scatter | solution.py:201
  785.5 14.8 %reduce-scatter.26.cloned.1.call-done = bf16[1024,768]{1,0:T(8,128)(2,1)} async-done(((bf16[2048,768]{1,0:T(8,128)(2,1)}), bf16[1024,768]{1,0:T(8,128)(2,1)}) %reduce-scatter.26.cloned.1.call-update) | async-done | bytes 1572880 | tf_op jit(solution)/shard_map/reduce_scatter | solution.py:204
  800.2 12.6 %reduce-scatter.16.cloned.1.call-done = bf16[384,768]{1,0:T(8,128)(2,1)} async-done(((bf16[768,768]{1,0:T(8,128)(2,1)}), bf16[384,768]{1,0:T(8,128)(2,1)}) %reduce-scatter.16.cloned.1.call-update) | async-done | bytes 589840 | tf_op jit(solution)/shard_map/reduce_scatter | solution.py:251
  812.8 12.6 %reduce-scatter.18.cloned.1.call-done = bf16[384,768]{1,0:T(8,128)(2,1)} async-done(((bf16[768,768]{1,0:T(8,128)(2,1)}), bf16[384,768]{1,0:T(8,128)(2,1)}) %reduce-scatter.18.cloned.1.call-update) | async-done | bytes 589840 | tf_op jit(solution)/shard_map/reduce_scatter | solution.py:254
  828.7 3.6 fusion.20
  833.5 2.5 all-reduce.4
  836.2 44.0 %all-reduce.2 = (bf16[384]{0:T(512)(128)(2,1)S(1)}, bf16[384]{0:T(512)(128)(2,1)S(1)}) all-reduce(bf16[384]{0:T(512)(128)(2,1)S(1)} %dynamic-slice.3, bf16[384]{0:T(512)(128)(2,1)S(1)} %dynamic-slice.5), channel_id=1, replica_groups=mesh['dp'=2,'ctx'=16] {'ctx'}, use_global_device_ids=true, to_apply=%region_11.12 | all-reduce | flops 768 | bytes 3072 | tf_op jit(solution)/shard_map/psum | solution.py:262
  882.3 184.2 %all-reduce.7.cloned.1.call-done = (bf16[384,768]{1,0:T(8,128)(2,1)}, bf16[384,768]{1,0:T(8,128)(2,1)}, bf16[384,768]{1,0:T(8,128)(2,1)}, bf16[384,768]{1,0:T(8,...) async-done(((bf16[384,768]{1,0:T(8,128)(2,1)}, bf16[384,768]{1,0:T(8,128)(2,1)}, bf16[384,768]{1,0:T(8,128)(2,1)}, ...) | async-done | bytes 7077904 | tf_op jit(solution)/shard_map/psum | solution.py:263
  1066.5 2.3 convert_element_type.247
  1068.8 2.2 convert_element_type.249
  1071.0 2.3 convert_element_type.251
  (170 shorter events, 58.7 us)
Async XLA Ops:
  7.2 26.3 %copy-start.1 = (bf16[1,256,768]{2,1,0:T(8,128)(2,1)S(1)}, bf16[1,256,768]{2,1,0:T(8,128)(2,1)}, u32[]{:S(2)}) copy-start(bf16[1,256,768]{2,1,0:T(8,128)(2,1)} %param.11) | copy-start | bytes 1179652
  7.2 14.3 %all-gather.16.cloned.1.call-start = ((), (), s32[]{:S(2)}) async-start(), calls=%async_computation.11 | async-start | bytes 1769472 | tf_op jit(solution)/shard_map/all_gather | solution.py:111
  7.9 25.6 %all-gather.12.cloned.1.call-start = ((), (), s32[]{:S(2)}) async-start(), calls=%async_computation.9 | async-start | bytes 1769472 | tf_op jit(solution)/shard_map/all_gather | solution.py:112
  8.7 185.7 %all-gather.14.cloned.1.call-start = ((), (), s32[]{:S(2)}) async-start(), calls=%async_computation.10 | async-start | bytes 1769472 | tf_op jit(solution)/shard_map/all_gather | solution.py:110
  9.4 246.6 %all-gather.26.cloned.1.call-start = ((), (), s32[]{:S(2)}) async-start(), calls=%async_computation.25 | async-start | bytes 6684672 | tf_op jit(solution)/shard_map/all_gather | solution.py:147
  12.1 184.8 %copy-start.26 = (f32[768]{0:T(1024)}, f32[768]{0:T(1024)S(1)}, u32[]{:S(2)}) copy-start(f32[768]{0:T(1024)S(1)} %reshape.299) | copy-start | bytes 9220
  13.2 157.8 %copy-start.30 = (f32[256]{0:T(256)}, f32[256]{0:T(256)S(1)}, u32[]{:S(2)}) copy-start(f32[256]{0:T(256)S(1)} %fusion.29) | copy-start | bytes 3076
  13.3 184.8 %copy-start.28 = (f32[256]{0:T(256)}, f32[256]{0:T(256)S(1)}, u32[]{:S(2)}) copy-start(f32[256]{0:T(256)S(1)} %fusion.47) | copy-start | bytes 3076
  24.2 302.6 %all-gather.18.cloned.1.call-start = ((), (), s32[]{:S(2)}) async-start(), calls=%async_computation.12 | async-start | bytes 1769472 | tf_op jit(solution)/shard_map/all_gather | solution.py:113
  24.8 304.2 %all-gather.20.cloned.1.call-start = ((), (), s32[]{:S(2)}) async-start(), calls=%async_computation.13 | async-start | bytes 4718592 | tf_op jit(solution)/shard_map/all_gather | solution.py:155
  25.4 307.9 %all-gather.22.cloned.1.call-start = ((), (), s32[]{:S(2)}) async-start(), calls=%async_computation.14 | async-start | bytes 4718592 | tf_op jit(solution)/shard_map/all_gather | solution.py:156
  26.1 311.3 %all-gather.24.cloned.1.call-start = ((), (), s32[]{:S(2)}) async-start(), calls=%async_computation.15 | async-start | bytes 4718592 | tf_op jit(solution)/shard_map/all_gather | solution.py:157
  35.3 15.0 %collective-permute-start = (bf16[1,256,768]{2,1,0:T(8,128)(2,1)S(1)}, bf16[1,256,768]{2,1,0:T(8,128)(2,1)S(1)}, u32[]{:S(2)}, u32[]{:S(2)}) collective-permute-start(bf16[1,256,768]{2,1,0:T(8,128)(2,1)S(1)} %bitcast.168), channel_id=1, source_target_pairs={{0,1},{1,2},{2,3},{3,4},{4,5},{5,6},{6,7},{7,8},{8,9},{9,10},{10,1... | collective-permute-start | bytes 1179656 | tf_op jit(solution)/shard_map/ppermute | solution.py:129
  50.3 19.6 %collective-permute-start.1 = (bf16[1,256,768]{2,1,0:T(8,128)(2,1)S(1)}, bf16[1,256,768]{2,1,0:T(8,128)(2,1)S(1)}, u32[]{:S(2)}, u32[]{:S(2)}) collective-permute-start(bf16[1,256,768]{2,1,0:T(8,128)(2,1)S(1)} %collective-permute-done), channel_id=1, source_target_pairs={{0,1},{1,2},{2,3},{3,4},{4,5},{5,6},{6,7},{7,8},{8,9},{9,10},{10,1... | collective-permute-start | bytes 1179656 | tf_op jit(solution)/shard_map/ppermute | solution.py:129
  50.3 22.1 %collective-permute-start.8 = (bf16[1,256,768]{2,1,0:T(8,128)(2,1)S(1)}, bf16[1,256,768]{2,1,0:T(8,128)(2,1)S(1)}, u32[]{:S(2)}, u32[]{:S(2)}) collective-permute-start(bf16[1,256,768]{2,1,0:T(8,128)(2,1)S(1)} %bitcast.169), channel_id=1, source_target_pairs={{1,0},{2,1},{3,2},{4,3},{5,4},{6,5},{7,6},{8,7},{9,8},{10,9},{11,1... | collective-permute-start | bytes 1179656 | tf_op jit(solution)/shard_map/ppermute | solution.py:134
  70.0 29.7 %collective-permute-start.2 = (bf16[1,256,768]{2,1,0:T(8,128)(2,1)S(1)}, bf16[1,256,768]{2,1,0:T(8,128)(2,1)S(1)}, u32[]{:S(2)}, u32[]{:S(2)}) collective-permute-start(bf16[1,256,768]{2,1,0:T(8,128)(2,1)S(1)} %collective-permute-done.1), channel_id=1, source_target_pairs={{0,1},{1,2},{2,3},{3,4},{4,5},{5,6},{6,7},{7,8},{8,9},{9,10},{10,1... | collective-permute-start | bytes 1179656 | tf_op jit(solution)/shard_map/ppermute | solution.py:129
  72.4 32.1 %collective-permute-start.9 = (bf16[1,256,768]{2,1,0:T(8,128)(2,1)S(1)}, bf16[1,256,768]{2,1,0:T(8,128)(2,1)S(1)}, u32[]{:S(2)}, u32[]{:S(2)}) collective-permute-start(bf16[1,256,768]{2,1,0:T(8,128)(2,1)S(1)} %collective-permute-done.8), channel_id=1, source_target_pairs={{1,0},{2,1},{3,2},{4,3},{5,4},{6,5},{7,6},{8,7},{9,8},{10,9},{11,1... | collective-permute-start | bytes 1179656 | tf_op jit(solution)/shard_map/ppermute | solution.py:134
  99.7 16.9 %collective-permute-start.3 = (bf16[1,256,768]{2,1,0:T(8,128)(2,1)S(1)}, bf16[1,256,768]{2,1,0:T(8,128)(2,1)S(1)}, u32[]{:S(2)}, u32[]{:S(2)}) collective-permute-start(bf16[1,256,768]{2,1,0:T(8,128)(2,1)S(1)} %collective-permute-done.2), channel_id=1, source_target_pairs={{0,1},{1,2},{2,3},{3,4},{4,5},{5,6},{6,7},{7,8},{8,9},{9,10},{10,1... | collective-permute-start | bytes 1179656 | tf_op jit(solution)/shard_map/ppermute | solution.py:129
  104.5 18.4 %collective-permute-start.10 = (bf16[1,256,768]{2,1,0:T(8,128)(2,1)S(1)}, bf16[1,256,768]{2,1,0:T(8,128)(2,1)S(1)}, u32[]{:S(2)}, u32[]{:S(2)}) collective-permute-start(bf16[1,256,768]{2,1,0:T(8,128)(2,1)S(1)} %collective-permute-done.9), channel_id=1, source_target_pairs={{1,0},{2,1},{3,2},{4,3},{5,4},{6,5},{7,6},{8,7},{9,8},{10,9},{11,1... | collective-permute-start | bytes 1179656 | tf_op jit(solution)/shard_map/ppermute | solution.py:134
  116.6 29.6 %copy-start.24 = (bf16[1,256,768]{2,1,0:T(8,128)(2,1)}, bf16[1,256,768]{2,1,0:T(8,128)(2,1)S(1)}, u32[]{:S(2)}) copy-start(bf16[1,256,768]{2,1,0:T(8,128)(2,1)S(1)} %collective-permute-done.3) | copy-start | bytes 1179652
  116.6 24.0 %collective-permute-start.4 = (bf16[1,256,768]{2,1,0:T(8,128)(2,1)S(1)}, bf16[1,256,768]{2,1,0:T(8,128)(2,1)S(1)}, u32[]{:S(2)}, u32[]{:S(2)}) collective-permute-start(bf16[1,256,768]{2,1,0:T(8,128)(2,1)S(1)} %collective-permute-done.3), channel_id=1, source_target_pairs={{0,1},{1,2},{2,3},{3,4},{4,5},{5,6},{6,7},{7,8},{8,9},{9,10},{10,1... | collective-permute-start | bytes 1179656 | tf_op jit(solution)/shard_map/ppermute | solution.py:129
  122.9 23.2 %collective-permute-start.11 = (bf16[1,256,768]{2,1,0:T(8,128)(2,1)S(1)}, bf16[1,256,768]{2,1,0:T(8,128)(2,1)S(1)}, u32[]{:S(2)}, u32[]{:S(2)}) collective-permute-start(bf16[1,256,768]{2,1,0:T(8,128)(2,1)S(1)} %collective-permute-done.10), channel_id=1, source_target_pairs={{1,0},{2,1},{3,2},{4,3},{5,4},{6,5},{7,6},{8,7},{9,8},{10,9},{11,1... | collective-permute-start | bytes 1179656 | tf_op jit(solution)/shard_map/ppermute | solution.py:134
  140.6 15.2 %copy-start.25 = (bf16[1,256,768]{2,1,0:T(8,128)(2,1)}, bf16[1,256,768]{2,1,0:T(8,128)(2,1)S(1)}, u32[]{:S(2)}) copy-start(bf16[1,256,768]{2,1,0:T(8,128)(2,1)S(1)} %collective-permute-done.4) | copy-start | bytes 1179652
  140.6 26.7 %collective-permute-start.5 = (bf16[1,256,768]{2,1,0:T(8,128)(2,1)S(1)}, bf16[1,256,768]{2,1,0:T(8,128)(2,1)}, u32[]{:S(2)}, u32[]{:S(2)}) collective-permute-start(bf16[1,256,768]{2,1,0:T(8,128)(2,1)S(1)} %collective-permute-done.4), channel_id=1, source_target_pairs={{0,1},{1,2},{2,3},{3,4},{4,5},{5,6},{6,7},{7,8},{8,9},{9,10},{10,1... | collective-permute-start | bytes 1179656 | tf_op jit(solution)/shard_map/ppermute | solution.py:129
  146.2 48.2 %copy-start.22 = (bf16[1,256,768]{2,1,0:T(8,128)(2,1)}, bf16[1,256,768]{2,1,0:T(8,128)(2,1)S(1)}, u32[]{:S(2)}) copy-start(bf16[1,256,768]{2,1,0:T(8,128)(2,1)S(1)} %collective-permute-done.11) | copy-start | bytes 1179652
  146.2 29.3 %collective-permute-start.12 = (bf16[1,256,768]{2,1,0:T(8,128)(2,1)S(1)}, bf16[1,256,768]{2,1,0:T(8,128)(2,1)}, u32[]{:S(2)}, u32[]{:S(2)}) collective-permute-start(bf16[1,256,768]{2,1,0:T(8,128)(2,1)S(1)} %collective-permute-done.11), channel_id=1, source_target_pairs={{1,0},{2,1},{3,2},{4,3},{5,4},{6,5},{7,6},{8,7},{9,8},{10,9},{11,1... | collective-permute-start | bytes 1179656 | tf_op jit(solution)/shard_map/ppermute | solution.py:134
  167.2 23.5 %collective-permute-start.6 = (bf16[1,256,768]{2,1,0:T(8,128)(2,1)}, bf16[1,256,768]{2,1,0:T(8,128)(2,1)}, u32[]{:S(2)}, u32[]{:S(2)}) collective-permute-start(bf16[1,256,768]{2,1,0:T(8,128)(2,1)} %collective-permute-done.5), channel_id=1, source_target_pairs={{0,1},{1,2},{2,3},{3,4},{4,5},{5,6},{6,7},{7,8},{8,9},{9,10},{10,1... | collective-permute-start | bytes 1179656 | tf_op jit(solution)/shard_map/ppermute | solution.py:129
  170.3 411.8 %reduce-scatter.10.cloned.1.call-start = ((), (), s32[]{:S(2)}) async-start(), calls=%async_computation.16 | async-start | bytes 6684672 | tf_op jit(solution)/shard_map/reduce_scatter | solution.py:221
  175.5 22.7 %collective-permute-start.13 = (bf16[1,256,768]{2,1,0:T(8,128)(2,1)}, bf16[1,256,768]{2,1,0:T(8,128)(2,1)}, u32[]{:S(2)}, u32[]{:S(2)}) collective-permute-start(bf16[1,256,768]{2,1,0:T(8,128)(2,1)} %collective-permute-done.12), channel_id=1, source_target_pairs={{1,0},{2,1},{3,2},{4,3},{5,4},{6,5},{7,6},{8,7},{9,8},{10,9},{11,1... | collective-permute-start | bytes 1179656 | tf_op jit(solution)/shard_map/ppermute | solution.py:134
  190.7 19.2 %collective-permute-start.7 = (bf16[1,256,768]{2,1,0:T(8,128)(2,1)}, bf16[1,256,768]{2,1,0:T(8,128)(2,1)}, u32[]{:S(2)}, u32[]{:S(2)}) collective-permute-start(bf16[1,256,768]{2,1,0:T(8,128)(2,1)} %collective-permute-done.6), channel_id=1, source_target_pairs={{0,1},{1,2},{2,3},{3,4},{4,5},{5,6},{6,7},{7,8},{8,9},{9,10},{10,1... | collective-permute-start | bytes 1179656 | tf_op jit(solution)/shard_map/ppermute | solution.py:129
  198.1 66.5 %copy-start.4 = (bf16[256,768]{0,1:T(8,128)(2,1)}, bf16[256,768]{0,1:T(8,128)(2,1)S(1)}, u32[]{:S(2)}) copy-start(bf16[256,768]{0,1:T(8,128)(2,1)S(1)} %copy.35) | copy-start | bytes 1179652
  198.1 26.3 %copy-start.23 = (bf16[1,256,768]{2,1,0:T(8,128)(2,1)S(1)}, bf16[1,256,768]{2,1,0:T(8,128)(2,1)}, u32[]{:S(2)}) copy-start(bf16[1,256,768]{2,1,0:T(8,128)(2,1)} %copy-done.22) | copy-start | bytes 1179652
  198.1 30.6 %collective-permute-start.14 = (bf16[1,256,768]{2,1,0:T(8,128)(2,1)}, bf16[1,256,768]{2,1,0:T(8,128)(2,1)S(1)}, u32[]{:S(2)}, u32[]{:S(2)}) collective-permute-start(bf16[1,256,768]{2,1,0:T(8,128)(2,1)} %collective-permute-done.13), channel_id=1, source_target_pairs={{1,0},{2,1},{3,2},{4,3},{5,4},{6,5},{7,6},{8,7},{9,8},{10,9},{11,1... | collective-permute-start | bytes 1179656 | tf_op jit(solution)/shard_map/ppermute | solution.py:134
  286.8 20.8 %copy-start = (bf16[4096,12,64]{0,2,1:T(8,128)(2,1)S(1)}, bf16[4096,12,64]{0,2,1:T(8,128)(2,1)}, u32[]{:S(2)}) copy-start(bf16[4096,12,64]{0,2,1:T(8,128)(2,1)} %reshape.271) | copy-start | bytes 18874372
  328.8 8.6 copy-start.12
  337.4 6.7 copy-start.11
  337.5 7.7 copy-start.2
  344.1 2.5 copy-start.6
  344.1 2.5 copy-start.21
  344.1 2.5 copy-start.3
  382.4 40.1 %copy-start.5 = (bf16[256,768]{0,1:T(8,128)(2,1)S(1)}, bf16[256,768]{0,1:T(8,128)(2,1)}, u32[]{:S(2)}) copy-start(bf16[256,768]{0,1:T(8,128)(2,1)} %copy-done.4) | copy-start | bytes 1179652
  437.7 294.7 %reduce-scatter.12.cloned.1.call-start = ((), (), s32[]{:S(2)}) async-start(), calls=%async_computation.17 | async-start | bytes 6684672 | tf_op jit(solution)/shard_map/reduce_scatter | solution.py:224
  459.9 14.5 %copy-start.27 = (f32[768]{0:T(1024)S(1)}, f32[768]{0:T(1024)}, u32[]{:S(2)}) copy-start(f32[768]{0:T(1024)} %copy-done.26) | copy-start | bytes 9220
  459.9 14.5 %copy-start.29 = (f32[256]{0:T(256)S(1)}, f32[256]{0:T(256)}, u32[]{:S(2)}) copy-start(f32[256]{0:T(256)} %copy-done.28) | copy-start | bytes 3076
  459.9 283.1 %reduce-scatter.14.cloned.1.call-start = ((), (), s32[]{:S(2)}) async-start(), calls=%async_computation.18 | async-start | bytes 1769472 | tf_op jit(solution)/shard_map/reduce_scatter | solution.py:248
  476.1 6.7 copy-start.7
  476.1 279.6 %reduce-scatter.20.cloned.1.call-start = ((), (), s32[]{:S(2)}) async-start(), calls=%async_computation.21 | async-start | bytes 1769472 | tf_op jit(solution)/shard_map/reduce_scatter | solution.py:257
  478.7 291.9 %reduce-scatter.22.cloned.1.call-start = ((), (), s32[]{:S(2)}) async-start(), calls=%async_computation.22 | async-start | bytes 4718592 | tf_op jit(solution)/shard_map/reduce_scatter | solution.py:198
  482.7 302.8 %reduce-scatter.24.cloned.1.call-start = ((), (), s32[]{:S(2)}) async-start(), calls=%async_computation.23 | async-start | bytes 4718592 | tf_op jit(solution)/shard_map/reduce_scatter | solution.py:201
  485.5 314.8 %reduce-scatter.26.cloned.1.call-start = ((), (), s32[]{:S(2)}) async-start(), calls=%async_computation.24 | async-start | bytes 4718592 | tf_op jit(solution)/shard_map/reduce_scatter | solution.py:204
  489.6 335.9 %copy-start.32 = (u32[32]{0:T(128)S(1)}, u32[32]{0:T(128)}, u32[]{:S(2)}) copy-start(u32[32]{0:T(128)} %constant.97) | copy-start | bytes 388
  489.6 337.1 %copy-start.9 = (bf16[12,64,256]{2,1,0:T(8,128)(2,1)S(1)}, bf16[12,64,256]{2,1,0:T(8,128)(2,1)}, u32[]{:S(2)}) copy-start(bf16[12,64,256]{2,1,0:T(8,128)(2,1)} %copy-done.8) | copy-start | bytes 1179652
  489.6 323.3 %reduce-scatter.16.cloned.1.call-start = ((), (), s32[]{:S(2)}) async-start(), calls=%async_computation.19 | async-start | bytes 1769472 | tf_op jit(solution)/shard_map/reduce_scatter | solution.py:251
  584.8 243.9 %copy-start.10 = (bf16[256,2048]{1,0:T(8,128)(2,1)S(1)}, bf16[256,2048]{1,0:T(8,128)(2,1)}, u32[]{:S(2)}) copy-start(bf16[256,2048]{1,0:T(8,128)(2,1)} %get-tuple-element.73) | copy-start | bytes 3145732
  584.8 240.6 %reduce-scatter.18.cloned.1.call-start = ((), (), s32[]{:S(2)}) async-start(), calls=%async_computation.20 | async-start | bytes 1769472 | tf_op jit(solution)/shard_map/reduce_scatter | solution.py:254
  735.0 331.5 %all-reduce.7.cloned.1.call-start = ((), (), s32[]{:S(2)}) async-start(), calls=%async_computation.26 | async-start | bytes 14155776 | tf_op jit(solution)/shard_map/psum | solution.py:263
  826.7 5.6 copy-start.13
  826.7 5.6 copy-start.19
  826.7 6.1 copy-start.14
  826.7 6.1 copy-start.20
  828.7 52.6 %copy-start.31 = (f32[256]{0:T(256)S(1)}, f32[256]{0:T(256)}, u32[]{:S(2)}) copy-start(f32[256]{0:T(256)} %copy-done.30) | copy-start | bytes 3076
  1066.5 8.9 copy-start.18
  1066.5 10.9 %copy-start.17 = (bf16[384,2048]{1,0:T(8,128)(2,1)S(1)}, bf16[384,2048]{1,0:T(8,128)(2,1)}, u32[]{:S(2)}) copy-start(bf16[384,2048]{1,0:T(8,128)(2,1)} %get-tuple-element.67) | copy-start | bytes 4718596
  1071.0 8.5 copy-start.16
  (2 other events, 3.7 us)
Sparse Core Ops, SparseCore 0:
  9.6 11.9 all-gather.15
  23.1 10.3 all-gather.11
  35.0 10.3 all-gather.13
  48.7 146.7 all-gather.25
  196.9 18.6 all-gather.17
  216.9 13.2 all-gather.19
  231.8 13.2 all-gather.21
  246.7 13.2 all-gather.23
  437.8 144.2 reduce-scatter.9
  587.2 145.1 reduce-scatter.11
  735.2 7.7 reduce-scatter.13
  745.8 9.8 reduce-scatter.19
  758.5 12.0 reduce-scatter.21
  773.4 12.0 reduce-scatter.23
  788.1 12.0 reduce-scatter.25
  803.0 9.8 reduce-scatter.15
  815.5 9.8 reduce-scatter.17
  832.8 233.6 all-reduce.6
